TPU v7x, 32 devices: a whole 2x2x4 slice. The times are simulated.
32 devices in a mesh: dp: 2 (over y), fsdp: 16 (over z, x, core).
Axes of the slice: x: 2, y: 2, z: 4, core: 2. Of those that a mesh axis runs over, the one named last changes fastest.
Arguments:
- ids: int32 [2, 192], P('dp'), may hold values from 0 to 511
- embed: bfloat16 [512, 8192], P(None, 'fsdp'), may hold values from -32 to 32
- gain: bfloat16 [8192], P('fsdp'), may hold values from 0.099609375 to 1.8984375
- w_in: bfloat16 [3, 4096, 8192], P(None, 'fsdp'), may hold values from -0.0625 to 0.0625
- feat_filter: float32 [3, 256, 7], P(None, 'fsdp'), may hold values from -2.4 to 2.4
- inner_filter: float32 [256, 7], P('fsdp'), may hold values from -2.4 to 2.4
- w_out: bfloat16 [4096, 8192], P(None, 'fsdp'), may hold values from -0.09375 to 0.09375
- cotangent: bfloat16 [2, 192, 8192], P('dp', None, 'fsdp'), may hold values from -6 to 6
- right_prev: bfloat16 [8192, 256], P('fsdp'), may hold values from -6 to 6
Outputs:
- block_out: bfloat16 [2, 192, 8192], P('dp', None, 'fsdp')
- filter_grad: float32 [4, 256, 7], P(None, 'fsdp')
- basis: bfloat16 [4096, 256], P('fsdp')
- right_factor: float32 [8192, 256], P('fsdp')
All inputs are finite; a program needn't handle non-finite values.
Results may differ from a plain program's by a relative error of at most 0.014.
The roundings to bfloat16 on the way count: a program that leaves them out, or rounds other values in their place, can miss the bound.
Values may be sent and summed in bfloat16 or wider, within the bound.
No kernel may reach another device: no remote copies, remote signals or barrier semaphores. Data moves between devices by JAX's collectives and lax.ppermute only.
A program may use at most 128 MiB of HBM per device.

v0:
```python
import jax
import jax.numpy as jnp
from jax import lax
from jax.sharding import PartitionSpec as P

D = 8192
C = 4096
GROUP = 16


def shifted(signal, lag, tap_count):
    padded = jnp.pad(signal, ((tap_count - 1, 0), (0, 0)))
    first = tap_count - 1 - lag
    return padded[first : first + signal.shape[0]]


def causal(signal, tap_table):
    tap_count = tap_table.shape[0]
    result = jnp.zeros(signal.shape, jnp.float32)
    for lag in range(tap_count):
        result = result + tap_table[lag][None, :] * shifted(signal, lag, tap_count)
    return result


def anticausal(signal, tap_table):
    tap_count = tap_table.shape[0]
    padded = jnp.pad(signal, ((0, tap_count - 1), (0, 0)))
    result = jnp.zeros(signal.shape, jnp.float32)
    for lag in range(tap_count):
        result = result + tap_table[lag][None, :] * padded[lag : lag + signal.shape[0]]
    return result


def tap_sums(gradient, signal, tap_count):
    listing = []
    for lag in range(tap_count):
        listing.append(jnp.sum(gradient * shifted(signal, lag, tap_count), axis=0))
    stacked = jnp.stack(listing, axis=0)
    grouped = stacked.reshape(tap_count, stacked.shape[1] // GROUP, GROUP).sum(axis=2)
    return grouped.T


def expand(filters):
    return jnp.repeat(filters.T, GROUP, axis=1)


def per_device(ids, embed, gain, w_in, feat_filter, inner_filter, w_out, cotangent, right_prev):
    tokens = ids[0]
    length = tokens.shape[0]
    tap_count = inner_filter.shape[1]
    onehot = (tokens[:, None] == jnp.arange(embed.shape[0], dtype=jnp.int32)[None, :]).astype(
        jnp.bfloat16
    )
    x_cols = jnp.dot(onehot, embed, preferred_element_type=jnp.float32)
    square_sums = lax.psum(jnp.sum(x_cols * x_cols, axis=1), "fsdp")
    factor = lax.rsqrt(square_sums / D + 1e-05)
    normed_cols = (x_cols * factor[:, None] * gain.astype(jnp.float32)[None, :]).astype(
        jnp.bfloat16
    )
    projected = jnp.einsum(
        "ld,kcd->klc",
        lax.all_gather(normed_cols, "fsdp", axis=1, tiled=True),
        w_in,
        preferred_element_type=jnp.float32,
    )
    rounded = lax.optimization_barrier(projected.astype(jnp.bfloat16)).astype(jnp.float32)
    query, key_in, value = (rounded[0], rounded[1], rounded[2])
    query_conv = causal(query, expand(feat_filter[0]))
    key_conv = causal(key_in, expand(feat_filter[1]))
    value_conv = causal(value, expand(feat_filter[2]))
    gated = key_conv * value_conv
    inner_table = expand(inner_filter)
    window = causal(gated, inner_table)
    gated_out = (query_conv * window).astype(jnp.bfloat16)
    cot_cols = cotangent[0]
    shard_piece = lax.all_gather(gated_out, "fsdp", axis=1, tiled=True)
    weight_rows = w_out
    mixed_sum = jnp.dot(shard_piece, weight_rows, preferred_element_type=jnp.float32)
    term = jnp.einsum("lc,ld->cd", shard_piece, cot_cols, preferred_element_type=jnp.float32)
    mixed_sum, grad_part = (mixed_sum, term)
    block_out = (x_cols + mixed_sum).astype(jnp.bfloat16)[None]
    weight_rows = w_out
    mixed_grad = lax.psum_scatter(
        jnp.einsum("cd,ld->cl", weight_rows, cot_cols, preferred_element_type=jnp.float32),
        "fsdp",
        scatter_dimension=0,
        tiled=True,
    ).T
    query_grad = mixed_grad * window
    window_grad = mixed_grad * query_conv
    gated_grad = anticausal(window_grad, inner_table)
    key_grad = gated_grad * value_conv
    value_grad = gated_grad * key_conv
    norm_factor = 1.0 / jnp.sqrt(jnp.float32(lax.axis_size("dp") * length))
    filter_part = (
        jnp.stack(
            [
                tap_sums(query_grad, query, tap_count),
                tap_sums(key_grad, key_in, tap_count),
                tap_sums(value_grad, value, tap_count),
                tap_sums(window_grad, gated, tap_count),
            ],
            axis=0,
        )
        * norm_factor
    )
    grad_total, filter_grad = (
        lax.psum(grad_part.astype(jnp.bfloat16), "dp").astype(jnp.float32),
        lax.psum(filter_part.astype(jnp.bfloat16), "dp").astype(jnp.float32),
    )
    grad_half = grad_total.astype(jnp.bfloat16)
    grad_rows_own = lax.all_to_all(grad_half, "fsdp", split_axis=0, concat_axis=1, tiled=True)
    panel_own = jnp.dot(
        grad_rows_own,
        lax.all_gather(right_prev, "fsdp", axis=0, tiled=True),
        preferred_element_type=jnp.float32,
    ).astype(jnp.bfloat16)
    root_scale = jnp.sqrt(jnp.float32(C))
    gram_local = jnp.einsum("cr,cs->rs", panel_own, panel_own, preferred_element_type=jnp.float32)
    gram_matrix = lax.psum(gram_local, "fsdp")
    lower_factor = jnp.linalg.cholesky(gram_matrix)
    solved = jax.scipy.linalg.solve_triangular(
        lower_factor, panel_own.astype(jnp.float32).T, lower=True
    ).T
    basis_own = (solved * root_scale).astype(jnp.bfloat16)
    right_raw = jnp.einsum(
        "cd,cr->dr",
        grad_half,
        lax.all_gather(basis_own, "fsdp", axis=0, tiled=True),
        preferred_element_type=jnp.float32,
    )
    column_sums = lax.psum(jnp.sum(right_raw * right_raw, axis=0), "fsdp")
    right_factor = right_raw * lax.rsqrt(column_sums / D + 1e-06)[None, :]
    return (block_out, filter_grad, basis_own, right_factor)


def solution(mesh):
    placed = (
        P("dp", None),
        P(None, "fsdp"),
        P("fsdp"),
        P(None, "fsdp", None),
        P(None, "fsdp", None),
        P("fsdp", None),
        P(None, "fsdp"),
        P("dp", None, "fsdp"),
        P("fsdp", None),
    )
    return jax.shard_map(
        per_device,
        mesh=mesh,
        in_specs=placed,
        out_specs=(P("dp", None, "fsdp"), P(None, "fsdp", None), P("fsdp", None), P("fsdp", None)),
        check_vma=False,
    )
```

profile of v0, /device:TPU:0, one launch (start us, length us, event | category | flops | bytes accessed | tf_op | source)
XLA Modules:
  0.0 699.4 jit_solution(17935779332028869934)
XLA Ops:
  9.3 34.9 %psum.35 = f32[192]{0:T(256)S(1)} all-reduce(f32[192]{0:T(256)S(1)} %get-tuple-element.121), channel_id=1, replica_groups=mesh['dp'=2,'fsdp'=16] {'fsdp'}, use_global_device_ids=true, to_apply=%region_1.0 | all-reduce | flops 192 | bytes 1536 | tf_op jit(solution)/shard_map/psum | solution.py:55
  45.1 5.4 fusion.14
  55.0 34.7 %all-gather.5.cloned.1.call-done = bf16[192,8192]{1,0:T(8,128)(2,1)} async-done(((bf16[192,512]{1,0:T(8,128)(2,1)}), bf16[192,8192]{1,0:T(8,128)(2,1)}) %all-gather.5.cloned.1.call-update) | async-done | bytes 3145744 | tf_op jit(solution)/shard_map/all_gather | solution.py:62
  89.7 9.8 %fusion.6 = bf16[3,192,256]{2,1,0:T(8,128)(2,1)S(1)} fusion(bf16[3,256,8192]{2,1,0:T(8,128)(2,1)} %param.12, bf16[192,8192]{1,0:T(8,128)(2,1)} %all-gather.5.cloned.1.call-done), kind=kOutput, calls=%fused_computation.8 | convolution fusion | flops 2416066560 | bytes 16023552 | tf_op jit(solution)/shard_map/ld,kcd->klc/dot_general | solution.py:60
  99.6 58.3 %reduce-scatter.2.cloned.1.call-done = f32[256,192]{0,1:T(8,128)} async-done(((f32[4096,192]{0,1:T(8,128)}), f32[256,192]{0,1:T(8,128)}) %reduce-scatter.2.cloned.1.call-update) | async-done | bytes 196624 | tf_op jit(solution)/shard_map/reduce_scatter | solution.py:83
  161.0 2.6 multiply_reduce_fusion.23
  164.3 38.0 %all-gather.7.cloned.1.call-done = bf16[192,4096]{1,0:T(8,128)(2,1)} async-done(((bf16[192,256]{1,0:T(8,128)(2,1)}), bf16[192,4096]{1,0:T(8,128)(2,1)}) %all-gather.7.cloned.1.call-update) | async-done | bytes 1572880 | tf_op jit(solution)/shard_map/all_gather | solution.py:76
  202.3 4.7 convolution_convert_fusion
  207.7 106.5 %all-reduce.9.cloned.1.call-done = bf16[4096,512]{1,0:T(8,128)(2,1)} async-done(((bf16[4096,512]{1,0:T(8,128)(2,1)}), bf16[4096,512]{1,0:T(8,128)(2,1)}) %all-reduce.9.cloned.1.call-update) | async-done | bytes 4194320 | tf_op jit(solution)/shard_map/psum | solution.py:108
  314.2 6.4 copy.22
  320.6 5.7 all-to-all-start
  326.3 94.7 %all-gather.9.cloned.1.call-done = bf16[8192,256]{1,0:T(8,128)(2,1)} async-done(((bf16[512,256]{1,0:T(8,128)(2,1)}), bf16[8192,256]{1,0:T(8,128)(2,1)}) %all-gather.9.cloned.1.call-update) | async-done | bytes 4194320 | tf_op jit(solution)/shard_map/all_gather | solution.py:115
  421.0 6.5 all-to-all-done
  427.4 4.8 convolution_convert_fusion.1
  434.0 103.0 %all-reduce.11.cloned.1.call-done = f32[256,256]{0,1:T(8,128)} async-done(((f32[256,256]{0,1:T(8,128)}), f32[256,256]{0,1:T(8,128)}) %all-reduce.11.cloned.1.call-update) | async-done | bytes 262160 | tf_op jit(solution)/shard_map/psum | solution.py:120
  537.0 1.8 copy.24
  540.6 11.7 %cholesky.50 = f32[128,128]{1,0:T(8,128)S(1)} custom-call(f32[128,128]{1,0:T(8,128)S(1)} %cholesky.118), custom_call_target="Cholesky" | custom-call | tf_op jit(solution)/shard_map/jit(cholesky)/cholesky | solution.py:121
  553.6 9.8 %custom-call.15 = f32[1,128,128]{1,2,0:T(8,128)S(1)} custom-call(f32[1,128,128]{2,1,0:T(8,128)S(1)} %get-tuple-element.89), custom_call_target="InvertDiagBlocksLowerTriangular" | custom-call | tf_op jit(solution)/shard_map/jit(cholesky)/cholesky | solution.py:121
  563.4 1.7 constant_dynamic-update-slice_fusion.29
  566.2 11.7 %cholesky.105 = f32[128,128]{1,0:T(8,128)S(1)} custom-call(f32[128,128]{1,0:T(8,128)S(1)} %convolution_subtract_fusion.1), custom_call_target="Cholesky" | custom-call | tf_op jit(solution)/shard_map/jit(cholesky)/cholesky | solution.py:121
  581.7 1.7 select_select_fusion
  584.2 6.8 while.1
  584.8 2.9 bitcast_dynamic-update-slice_fusion.2
  588.2 2.8 bitcast_dynamic-update-slice_fusion.2
  591.0 20.5 %custom-call.16 = f32[2,128,128]{1,2,0:T(8,128)S(1)} custom-call(f32[2,128,128]{2,1,0:T(8,128)} %get-tuple-element.11), custom_call_target="InvertDiagBlocksLowerTriangular" | custom-call | tf_op jit(solution)/shard_map/jit(_solve_triangular)/triangular_solve | solution.py:122
  614.0 1.9 multiply_reduce_fusion.2
  616.6 2.0 multiply_reduce_fusion.29
  622.1 5.0 psum.36
  627.8 3.8 fusion.9
  632.4 23.5 %all-gather.11.cloned.1.call-done = bf16[4096,256]{0,1:T(8,128)(2,1)} async-done(((bf16[256,256]{0,1:T(8,128)(2,1)}), bf16[4096,256]{0,1:T(8,128)(2,1)}) %all-gather.11.cloned.1.call-update) | async-done | bytes 2097168 | tf_op jit(solution)/shard_map/all_gather | solution.py:129
  655.9 4.2 multiply_reduce_fusion
  660.1 31.6 %psum.39 = f32[256]{0:T(256)S(1)} all-reduce(f32[256]{0:T(256)S(1)} %get-tuple-element.125), channel_id=1, replica_groups=mesh['dp'=2,'fsdp'=16] {'fsdp'}, use_global_device_ids=true, to_apply=%region_43.44 | all-reduce | flops 256 | bytes 2048 | tf_op jit(solution)/shard_map/psum | solution.py:132
  (190 shorter events, 31.1 us)
Async XLA Ops:
  7.2 1.1 copy-start
  7.2 82.5 %all-gather.5.cloned.1.call-start = ((), (), s32[]{:S(2)}) async-start(), calls=%async_computation.2 | async-start | bytes 3342336 | tf_op jit(solution)/shard_map/all_gather | solution.py:62
  45.0 5.5 copy-start.8
  45.0 6.6 copy-start.9
  45.1 112.9 %reduce-scatter.2.cloned.1.call-start = ((), (), s32[]{:S(2)}) async-start(), calls=%async_computation.4 | async-start | bytes 3342336 | tf_op jit(solution)/shard_map/reduce_scatter | solution.py:83
  50.5 151.8 %all-gather.7.cloned.1.call-start = ((), (), s32[]{:S(2)}) async-start(), calls=%async_computation.3 | async-start | bytes 1671168 | tf_op jit(solution)/shard_map/all_gather | solution.py:76
  99.5 102.8 %copy-start.7 = (bf16[1,192,512]{2,1,0:T(8,128)(2,1)S(1)}, bf16[1,192,512]{2,1,0:T(8,128)(2,1)}, u32[]{:S(2)}) copy-start(bf16[1,192,512]{2,1,0:T(8,128)(2,1)} %param.16) | copy-start | bytes 589828
  99.6 61.3 %copy-start.3 = (f32[192,256]{1,0:T(8,128)}, f32[192,256]{1,0:T(8,128)S(1)}, u32[]{:S(2)}) copy-start(f32[192,256]{1,0:T(8,128)S(1)} %get-tuple-element.84) | copy-start | bytes 589828
  159.1 48.0 %copy-start.4 = (f32[192,256]{1,0:T(8,128)}, f32[192,256]{1,0:T(8,128)S(1)}, u32[]{:S(2)}) copy-start(f32[192,256]{1,0:T(8,128)S(1)} %get-tuple-element.79) | copy-start | bytes 589828
  161.0 46.1 %copy-start.2 = (f32[192,256]{1,0:T(8,128)}, f32[192,256]{1,0:T(8,128)S(1)}, u32[]{:S(2)}) copy-start(f32[192,256]{1,0:T(8,128)S(1)} %mul.459) | copy-start | bytes 589828
  164.2 150.0 %all-reduce.9.cloned.1.call-start = ((), (), s32[]{:S(2)}) async-start(), calls=%async_computation.5 | async-start | bytes 8388608 | tf_op jit(solution)/shard_map/psum | solution.py:108
  207.1 213.9 %all-gather.9.cloned.1.call-start = ((), (), s32[]{:S(2)}) async-start(), calls=%async_computation.6 | async-start | bytes 4456448 | tf_op jit(solution)/shard_map/all_gather | solution.py:115
  320.6 106.8 %all-to-all-start = ((bf16[16,256,512]{1,2,0:T(8,128)(2,1)}), bf16[16,256,512]{1,2,0:T(8,128)(2,1)}, u32[]{:S(2)}, u32[]{:S(2)}) async-start(bf16[16,256,512]{1,2,0:T(8,128)(2,1)} %copy.22), calls=%async_computation.1 | async-start | bytes 8388608 | tf_op jit(solution)/shard_map/all_to_all | solution.py:112
  326.2 210.8 %all-reduce.11.cloned.1.call-start = ((), (), s32[]{:S(2)}) async-start(), calls=%async_computation.7 | async-start | bytes 524288 | tf_op jit(solution)/shard_map/psum | solution.py:120
  433.2 222.7 %all-gather.11.cloned.1.call-start = ((), (), s32[]{:S(2)}) async-start(), calls=%async_computation.8 | async-start | bytes 2228224 | tf_op jit(solution)/shard_map/all_gather | solution.py:129
  434.0 193.8 %copy-start.1 = (bf16[192,4096]{1,0:T(8,128)(2,1)S(1)}, bf16[192,4096]{1,0:T(8,128)(2,1)}, u32[]{:S(2)}) copy-start(bf16[192,4096]{1,0:T(8,128)(2,1)} %all-gather.7.cloned.1.call-done) | copy-start | bytes 4718596
  539.9 0.7 copy-start.6
  616.6 15.0 %copy-start.5 = (bf16[256,256]{0,1:T(8,128)(2,1)S(1)}, bf16[256,256]{0,1:T(8,128)(2,1)}, u32[]{:S(2)}) copy-start(bf16[256,256]{0,1:T(8,128)(2,1)} %fusion.19) | copy-start | bytes 393220
Sparse Core Ops, SparseCore 0:
  45.2 44.4 all-gather.4
  93.5 64.4 reduce-scatter.1
  164.4 37.9 all-gather.6
  207.2 106.9 all-reduce.8
  316.4 104.4 all-gather.8
  433.3 103.7 all-reduce.10
  614.1 41.7 all-gather.10
where the time goes:
time: 700 us; the launch traced here: 699 us
  waiting for transfers between devices  466 us (67%)
  other arithmetic  73.8 us (11%)
  blocking collectives  71.5 us (10%)
  matrix products  39.3 us (6%)
  local copies, waits for them, and re-layouts  26.9 us (4%)
  between operations  15.8 us (2%)
    psum x1, waiting for transfers between devices, per_device(): lax.psum(grad_part.astype(jnp.bfloat16), 'dp').astype(jnp.float32)  107 us
    psum x1, waiting for transfers between devices, per_device(): gram_matrix = lax.psum(gram_local, 'fsdp')  103 us
    all_gather x1, waiting for transfers between devices, per_device(): lax.all_gather(right_prev, 'fsdp', axis=0, tiled=True)  94.7 us
    reduce_scatter x1, waiting for transfers between devices, per_device(): lax.psum_scatter(jnp.einsum('cd,ld->cl', weight_rows, cot_cols, preferred...  58.3 us
    all_gather x1, waiting for transfers between devices, per_device(): shard_piece = lax.all_gather(gated_out, 'fsdp', axis=1, tiled=True)  38 us
    another operation x7, other arithmetic, per_device(): lower_factor = jnp.linalg.cholesky(gram_matrix)  36.4 us
    psum x1, blocking collectives, per_device(): square_sums = lax.psum(jnp.sum(x_cols * x_cols, axis=1), 'fsdp')  34.9 us
    all_gather x1, waiting for transfers between devices, per_device(): lax.all_gather(normed_cols, 'fsdp', axis=1, tiled=True)  34.7 us
  transfers between devices with their start and end apart: 8, of which 8 were waited for; matrix products, arithmetic and copies ran while one was open for 6% of the time, Pallas kernels for 0%

commit v1 on v0

--- a/solution.py
+++ b/solution.py
@@ -117,7 +117,11 @@
     ).astype(jnp.bfloat16)
     root_scale = jnp.sqrt(jnp.float32(C))
     gram_local = jnp.einsum("cr,cs->rs", panel_own, panel_own, preferred_element_type=jnp.float32)
-    gram_matrix = lax.psum(gram_local, "fsdp")
+    gram_matrix = gram_local
+    for hop in (1, 2, 4, 8):
+        gram_matrix = gram_matrix + lax.ppermute(
+            gram_matrix, "fsdp", [(dev, dev ^ hop) for dev in range(16)]
+        )
     lower_factor = jnp.linalg.cholesky(gram_matrix)
     solved = jax.scipy.linalg.solve_triangular(
         lower_factor, panel_own.astype(jnp.float32).T, lower=True

time: 700 us -> 643 us (0.919)
  waiting for transfers between devices: 466 us -> 386 us
  starting transfers between devices: 6.13 us -> 27.2 us
    psum x1 -> x0, waiting for transfers between devices: 103 us -> none  [per_device(): gram_matrix = lax.psum(gram_local, 'fsdp')]
    ppermute x0 -> x4, waiting for transfers between devices: none -> 24.6 us  [per_device(): lax.ppermute(gram_matrix, 'fsdp', [(dev, dev ^ hop) for dev in range(16)])]
    ppermute x0 -> x4, starting transfers between devices: none -> 21.1 us  [per_device(): lax.ppermute(gram_matrix, 'fsdp', [(dev, dev ^ hop) for dev in range(16)])]
  transfers between devices with their start and end apart: 8 -> 11, of which waited for: 8 -> 11; matrix products, arithmetic and copies ran while one was open for 6% -> 6% of each run, Pallas kernels for 0% -> 0%
where the time goes in v1:
time: 643 us; the launch traced here: 642 us
  waiting for transfers between devices  386 us (60%)
  other arithmetic  75.2 us (12%)
  blocking collectives  71.5 us (11%)
  matrix products  40.3 us (6%)
  starting transfers between devices  27.2 us (4%)
  local copies, waits for them, and re-layouts  25.9 us (4%)
  between operations  15.9 us (2%)
    psum x1, waiting for transfers between devices, per_device(): lax.psum(grad_part.astype(jnp.bfloat16), 'dp').astype(jnp.float32)  107 us
    all_gather x1, waiting for transfers between devices, per_device(): lax.all_gather(right_prev, 'fsdp', axis=0, tiled=True)  94.5 us
    reduce_scatter x1, waiting for transfers between devices, per_device(): lax.psum_scatter(jnp.einsum('cd,ld->cl', weight_rows, cot_cols, preferred...  58.3 us
    all_gather x1, waiting for transfers between devices, per_device(): shard_piece = lax.all_gather(gated_out, 'fsdp', axis=1, tiled=True)  38 us
    another operation x7, other arithmetic, per_device(): lower_factor = jnp.linalg.cholesky(gram_matrix)  37.1 us
    psum x1, blocking collectives, per_device(): square_sums = lax.psum(jnp.sum(x_cols * x_cols, axis=1), 'fsdp')  34.9 us
    all_gather x1, waiting for transfers between devices, per_device(): lax.all_gather(normed_cols, 'fsdp', axis=1, tiled=True)  34.7 us
    psum x1, blocking collectives, per_device(): column_sums = lax.psum(jnp.sum(right_raw * right_raw, axis=0), 'fsdp')  31.6 us
  transfers between devices with their start and end apart: 11, of which 11 were waited for; matrix products, arithmetic and copies ran while one was open for 6% of the time, Pallas kernels for 0%

profile of v1, /device:TPU:0, one launch (start us, length us, event | category | flops | bytes accessed | tf_op | source)
XLA Modules:
  0.0 642.2 jit_solution(10323132610793809353)
XLA Ops:
  9.3 34.9 %psum.28 = f32[192]{0:T(256)S(1)} all-reduce(f32[192]{0:T(256)S(1)} %get-tuple-element.121), channel_id=1, replica_groups=mesh['dp'=2,'fsdp'=16] {'fsdp'}, use_global_device_ids=true, to_apply=%region_1.0 | all-reduce | flops 192 | bytes 1536 | tf_op jit(solution)/shard_map/psum | solution.py:55
  45.1 5.4 fusion.14
  55.0 34.7 %all-gather.5.cloned.1.call-done = bf16[192,8192]{1,0:T(8,128)(2,1)} async-done(((bf16[192,512]{1,0:T(8,128)(2,1)}), bf16[192,8192]{1,0:T(8,128)(2,1)}) %all-gather.5.cloned.1.call-update) | async-done | bytes 3145744 | tf_op jit(solution)/shard_map/all_gather | solution.py:62
  89.7 9.8 %fusion.6 = bf16[3,192,256]{2,1,0:T(8,128)(2,1)S(1)} fusion(bf16[3,256,8192]{2,1,0:T(8,128)(2,1)} %param.12, bf16[192,8192]{1,0:T(8,128)(2,1)} %all-gather.5.cloned.1.call-done), kind=kOutput, calls=%fused_computation.8 | convolution fusion | flops 2416066560 | bytes 16023552 | tf_op jit(solution)/shard_map/ld,kcd->klc/dot_general | solution.py:60
  99.6 58.3 %reduce-scatter.2.cloned.1.call-done = f32[256,192]{0,1:T(8,128)} async-done(((f32[4096,192]{0,1:T(8,128)}), f32[256,192]{0,1:T(8,128)}) %reduce-scatter.2.cloned.1.call-update) | async-done | bytes 196624 | tf_op jit(solution)/shard_map/reduce_scatter | solution.py:83
  161.0 2.6 multiply_reduce_fusion.23
  164.3 38.0 %all-gather.7.cloned.1.call-done = bf16[192,4096]{1,0:T(8,128)(2,1)} async-done(((bf16[192,256]{1,0:T(8,128)(2,1)}), bf16[192,4096]{1,0:T(8,128)(2,1)}) %all-gather.7.cloned.1.call-update) | async-done | bytes 1572880 | tf_op jit(solution)/shard_map/all_gather | solution.py:76
  202.3 4.7 convolution_convert_fusion
  207.7 106.5 %all-reduce.8.cloned.1.call-done = bf16[4096,512]{1,0:T(8,128)(2,1)} async-done(((bf16[4096,512]{1,0:T(8,128)(2,1)}), bf16[4096,512]{1,0:T(8,128)(2,1)}) %all-reduce.8.cloned.1.call-update) | async-done | bytes 4194320 | tf_op jit(solution)/shard_map/psum | solution.py:108
  314.2 6.4 copy.24
  320.6 5.7 all-to-all-start
  326.5 94.5 %all-gather.9.cloned.1.call-done = bf16[8192,256]{1,0:T(8,128)(2,1)} async-done(((bf16[512,256]{1,0:T(8,128)(2,1)}), bf16[8192,256]{1,0:T(8,128)(2,1)}) %all-gather.9.cloned.1.call-update) | async-done | bytes 4194320 | tf_op jit(solution)/shard_map/all_gather | solution.py:115
  421.0 6.5 %all-to-all-done = bf16[16,256,512]{1,2,0:T(8,128)(2,1)} async-done(((bf16[16,256,512]{1,2,0:T(8,128)(2,1)}), bf16[16,256,512]{1,2,0:T(8,128)(2,1)}, u32[]{:S(2)}, u32[]{:S(2)}) %all-to-all-start) | async-done | bytes 4194336 | tf_op jit(solution)/shard_map/all_to_all | solution.py:112
  427.4 4.8 convolution_convert_fusion.1
  434.1 6.2 collective-permute-start.1
  440.3 6.7 %collective-permute-done.1 = f32[256,256]{0,1:T(8,128)S(1)} collective-permute-done((f32[256,256]{0,1:T(8,128)S(1)}, f32[256,256]{0,1:T(8,128)S(1)}, u32[]{:S(2)}, u32[]{:S(2)}) %collective-permute-start.1) | collective-permute-done | bytes 262176 | tf_op jit(solution)/shard_map/ppermute | solution.py:122
  447.1 11.8 %collective-permute-start.2 = (f32[256,256]{0,1:T(8,128)S(1)}, f32[256,256]{0,1:T(8,128)S(1)}, u32[]{:S(2)}, u32[]{:S(2)}) collective-permute-start(f32[256,256]{0,1:T(8,128)S(1)} %add.194), channel_id=1, source_target_pairs={{0,4},{1,5},{2,6},{3,7},{4,0},{5,1},{6,2},{7,3},{8,12},{9,13},{10,... | collective-permute-start | bytes 786440 | tf_op jit(solution)/shard_map/ppermute | solution.py:122
  458.8 6.1 collective-permute-done.2
  465.0 2.7 collective-permute-start.3
  468.3 10.5 %collective-permute-done.3 = f32[256,256]{0,1:T(8,128)S(1)} collective-permute-done((f32[256,256]{0,1:T(8,128)S(1)}, f32[256,256]{0,1:T(8,128)S(1)}, u32[]{:S(2)}, u32[]{:S(2)}) %collective-permute-start.3) | collective-permute-done | bytes 262176 | tf_op jit(solution)/shard_map/ppermute | solution.py:122
  481.4 11.7 %cholesky.50 = f32[128,128]{1,0:T(8,128)S(1)} custom-call(f32[128,128]{1,0:T(8,128)S(1)} %cholesky.118), custom_call_target="Cholesky" | custom-call | tf_op jit(solution)/shard_map/jit(cholesky)/cholesky | solution.py:125
  494.4 10.4 %custom-call.15 = f32[1,128,128]{1,2,0:T(8,128)} custom-call(f32[1,128,128]{2,1,0:T(8,128)S(1)} %get-tuple-element.89), custom_call_target="InvertDiagBlocksLowerTriangular" | custom-call | tf_op jit(solution)/shard_map/jit(cholesky)/cholesky | solution.py:125
  507.7 11.7 %cholesky.105 = f32[128,128]{1,0:T(8,128)S(1)} custom-call(f32[128,128]{1,0:T(8,128)S(1)} %slice_subtract_fusion), custom_call_target="Cholesky" | custom-call | tf_op jit(solution)/shard_map/jit(cholesky)/cholesky | solution.py:125
  525.6 6.8 %while.1 = (s32[]{:T(128)}, f32[256,256]{1,0:T(8,128)}, s32[2,2]{1,0:T(2,128)S(1)}, f32[2,128,128]{2,1,0:T(8,128)}, s32[]{:T(128)}) while((s32[]{:T(128)}, f32[256,256]{1,0:T(8,128)}, s32[2,2]{1,0:T(2,128)S(1)}, f32[2,128,128]{2,1,0:T(8,128)}, s32[]{:T(128)}) %tuple.107), condition=%wide.while_cond, body=%wide.while_body.sunk | while | flops 2 | bytes 132205 | solution.py:126
  526.2 2.9 bitcast_dynamic-update-slice_fusion.2
  529.7 2.8 bitcast_dynamic-update-slice_fusion.2
  532.5 21.1 %custom-call.16 = f32[2,128,128]{1,2,0:T(8,128)} custom-call(f32[2,128,128]{2,1,0:T(8,128)} %get-tuple-element.11), custom_call_target="InvertDiagBlocksLowerTriangular" | custom-call | tf_op jit(solution)/shard_map/jit(_solve_triangular)/triangular_solve | solution.py:126
  566.0 5.0 psum.29
  571.6 3.8 fusion.9
  576.2 22.5 %all-gather.11.cloned.1.call-done = bf16[4096,256]{0,1:T(8,128)(2,1)} async-done(((bf16[256,256]{0,1:T(8,128)(2,1)}), bf16[4096,256]{0,1:T(8,128)(2,1)}) %all-gather.11.cloned.1.call-update) | async-done | bytes 2097168 | tf_op jit(solution)/shard_map/all_gather | solution.py:133
  598.8 4.2 multiply_reduce_fusion
  602.9 31.6 %psum.31 = f32[256]{0:T(256)S(1)} all-reduce(f32[256]{0:T(256)S(1)} %get-tuple-element.125), channel_id=1, replica_groups=mesh['dp'=2,'fsdp'=16] {'fsdp'}, use_global_device_ids=true, to_apply=%region_42.43 | all-reduce | flops 256 | bytes 2048 | tf_op jit(solution)/shard_map/psum | solution.py:136
  (203 shorter events, 41.8 us)
Async XLA Ops:
  7.2 1.1 copy-start
  7.2 82.5 %all-gather.5.cloned.1.call-start = ((), (), s32[]{:S(2)}) async-start(), calls=%async_computation.2 | async-start | bytes 3342336 | tf_op jit(solution)/shard_map/all_gather | solution.py:62
  45.0 5.5 copy-start.10
  45.0 6.6 %copy-start.11 = (f32[16,7]{0,1:T(8,128)S(1)}, f32[16,7]{0,1:T(8,128)}, u32[]{:S(2)}) copy-start(f32[16,7]{0,1:T(8,128)} %param.14) | copy-start | bytes 1348
  45.1 112.9 %reduce-scatter.2.cloned.1.call-start = ((), (), s32[]{:S(2)}) async-start(), calls=%async_computation.4 | async-start | bytes 3342336 | tf_op jit(solution)/shard_map/reduce_scatter | solution.py:83
  50.5 151.8 %all-gather.7.cloned.1.call-start = ((), (), s32[]{:S(2)}) async-start(), calls=%async_computation.3 | async-start | bytes 1671168 | tf_op jit(solution)/shard_map/all_gather | solution.py:76
  99.5 102.8 %copy-start.9 = (bf16[1,192,512]{2,1,0:T(8,128)(2,1)S(1)}, bf16[1,192,512]{2,1,0:T(8,128)(2,1)}, u32[]{:S(2)}) copy-start(bf16[1,192,512]{2,1,0:T(8,128)(2,1)} %param.16) | copy-start | bytes 589828
  99.6 61.3 %copy-start.5 = (f32[192,256]{1,0:T(8,128)}, f32[192,256]{1,0:T(8,128)S(1)}, u32[]{:S(2)}) copy-start(f32[192,256]{1,0:T(8,128)S(1)} %get-tuple-element.84) | copy-start | bytes 589828
  99.6 107.4 %copy-start.2 = (f32[192,256]{1,0:T(8,128)}, f32[192,256]{1,0:T(8,128)S(1)}, u32[]{:S(2)}) copy-start(f32[192,256]{1,0:T(8,128)S(1)} %get-tuple-element.83) | copy-start | bytes 589828
  159.1 48.0 %copy-start.6 = (f32[192,256]{1,0:T(8,128)}, f32[192,256]{1,0:T(8,128)S(1)}, u32[]{:S(2)}) copy-start(f32[192,256]{1,0:T(8,128)S(1)} %get-tuple-element.79) | copy-start | bytes 589828
  161.0 46.1 %copy-start.4 = (f32[192,256]{1,0:T(8,128)}, f32[192,256]{1,0:T(8,128)S(1)}, u32[]{:S(2)}) copy-start(f32[192,256]{1,0:T(8,128)S(1)} %mul.459) | copy-start | bytes 589828
  164.2 150.0 %all-reduce.8.cloned.1.call-start = ((), (), s32[]{:S(2)}) async-start(), calls=%async_computation.5 | async-start | bytes 8388608 | tf_op jit(solution)/shard_map/psum | solution.py:108
  207.1 213.9 %all-gather.9.cloned.1.call-start = ((), (), s32[]{:S(2)}) async-start(), calls=%async_computation.6 | async-start | bytes 4456448 | tf_op jit(solution)/shard_map/all_gather | solution.py:115
  320.6 106.8 %all-to-all-start = ((bf16[16,256,512]{1,2,0:T(8,128)(2,1)}), bf16[16,256,512]{1,2,0:T(8,128)(2,1)}, u32[]{:S(2)}, u32[]{:S(2)}) async-start(bf16[16,256,512]{1,2,0:T(8,128)(2,1)} %copy.24), calls=%async_computation.1 | async-start | bytes 8388608 | tf_op jit(solution)/shard_map/all_to_all | solution.py:112
  326.3 272.5 %all-gather.11.cloned.1.call-start = ((), (), s32[]{:S(2)}) async-start(), calls=%async_computation.7 | async-start | bytes 2228224 | tf_op jit(solution)/shard_map/all_gather | solution.py:133
  432.4 1.6 collective-permute-start
  434.1 13.0 %collective-permute-start.1 = (f32[256,256]{0,1:T(8,128)S(1)}, f32[256,256]{0,1:T(8,128)S(1)}, u32[]{:S(2)}, u32[]{:S(2)}) collective-permute-start(f32[256,256]{0,1:T(8,128)S(1)} %add.193), channel_id=1, source_target_pairs={{0,2},{1,3},{2,0},{3,1},{4,6},{5,7},{6,4},{7,5},{8,10},{9,11},{10,... | collective-permute-start | bytes 786440 | tf_op jit(solution)/shard_map/ppermute | solution.py:122
  447.1 17.9 %collective-permute-start.2 = (f32[256,256]{0,1:T(8,128)S(1)}, f32[256,256]{0,1:T(8,128)S(1)}, u32[]{:S(2)}, u32[]{:S(2)}) collective-permute-start(f32[256,256]{0,1:T(8,128)S(1)} %add.194), channel_id=1, source_target_pairs={{0,4},{1,5},{2,6},{3,7},{4,0},{5,1},{6,2},{7,3},{8,12},{9,13},{10,... | collective-permute-start | bytes 786440 | tf_op jit(solution)/shard_map/ppermute | solution.py:122
  465.0 13.8 %collective-permute-start.3 = (f32[256,256]{0,1:T(8,128)S(1)}, f32[256,256]{0,1:T(8,128)S(1)}, u32[]{:S(2)}, u32[]{:S(2)}) collective-permute-start(f32[256,256]{0,1:T(8,128)S(1)} %add.195), channel_id=1, source_target_pairs={{0,8},{1,9},{2,10},{3,11},{4,12},{5,13},{6,14},{7,15},{8,0},{9,1},... | collective-permute-start | bytes 786440 | tf_op jit(solution)/shard_map/ppermute | solution.py:122
  478.9 92.8 %copy-start.1 = (bf16[192,4096]{1,0:T(8,128)(2,1)S(1)}, bf16[192,4096]{1,0:T(8,128)(2,1)}, u32[]{:S(2)}) copy-start(bf16[192,4096]{1,0:T(8,128)(2,1)} %all-gather.7.cloned.1.call-done) | copy-start | bytes 4718596
  480.7 0.7 copy-start.8
  481.4 79.0 %copy-start.3 = (f32[192,256]{1,0:T(8,128)S(1)}, f32[192,256]{1,0:T(8,128)}, u32[]{:S(2)}) copy-start(f32[192,256]{1,0:T(8,128)} %copy-done.2) | copy-start | bytes 589828
  560.5 15.0 %copy-start.7 = (bf16[256,256]{0,1:T(8,128)(2,1)S(1)}, bf16[256,256]{0,1:T(8,128)(2,1)}, u32[]{:S(2)}) copy-start(bf16[256,256]{0,1:T(8,128)(2,1)} %fusion.19) | copy-start | bytes 393220
Sparse Core Ops, SparseCore 0:
  45.2 44.4 all-gather.4
  93.5 64.4 reduce-scatter.1
  164.4 37.9 all-gather.6
  207.2 106.9 all-reduce.7
  316.5 104.4 all-gather.8
  557.9 40.8 all-gather.10
